TPU v7x, 32 devices: a whole 2x2x4 slice. The times are simulated.
32 devices in a mesh: dp: 8 (over y, x, core), mem: 4 (over z).
Axes of the slice: x: 2, y: 2, z: 4, core: 2. Of those that a mesh axis runs over, the one named last changes fastest.
Arguments:
- inputs: bfloat16 [32, 100, 768], P('dp'), may hold values from -6 to 6
- memory: bfloat16 [32, 1280, 768], P('dp', 'mem'), may hold values from -6 to 6
- lengths: int32 [32], P('dp'), may hold values from 1 to 1280, as said below
- self_query: bfloat16 [768, 768], P('dp'), may hold values from -0.21875 to 0.21875
- self_key: bfloat16 [768, 768], P('dp'), may hold values from -0.21875 to 0.21875
- self_value: bfloat16 [768, 768], P('dp'), may hold values from -0.21875 to 0.21875
- self_out: bfloat16 [768, 768], P('dp'), may hold values from -0.625 to 0.625
- cross_query: bfloat16 [768, 768], P('dp'), may hold values from -0.21875 to 0.21875
- cross_key: bfloat16 [768, 768], P('dp'), may hold values from -0.21875 to 0.21875
- cross_value: bfloat16 [768, 768], P('dp'), may hold values from -0.21875 to 0.21875
- cross_out: bfloat16 [768, 768], P('dp'), may hold values from -1 to 1
- expand_weight: bfloat16 [768, 3072], P('dp'), may hold values from -0.21875 to 0.21875
- contract_weight: bfloat16 [3072, 768], P('dp'), may hold values from -0.109375 to 0.109375
- gain_one: float32 [768], replicated, may hold values from 0.5 to 1.5
- shift_one: float32 [768], replicated, may hold values from -1.5 to 1.5
- gain_two: float32 [768], replicated, may hold values from 0.5 to 1.5
- shift_two: float32 [768], replicated, may hold values from -1.5 to 1.5
- gain_three: float32 [768], replicated, may hold values from 0.5 to 1.5
- shift_three: float32 [768], replicated, may hold values from -1.5 to 1.5
- cotangent: bfloat16 [32, 100, 768], P('dp'), may hold values from -6 to 6
Outputs:
- output: float32 [32, 100, 768], P('dp')
- input_grad: float32 [32, 100, 768], P('dp')
- memory_grad: float32 [32, 1280, 768], P('dp', 'mem')
- self_query_grad: float32 [768, 768], P('dp')
- self_key_grad: float32 [768, 768], P('dp')
- self_value_grad: float32 [768, 768], P('dp')
- self_out_grad: float32 [768, 768], P('dp')
- cross_query_grad: float32 [768, 768], P('dp')
- cross_key_grad: float32 [768, 768], P(('dp', 'mem'))
- cross_value_grad: float32 [768, 768], P(('dp', 'mem'))
- cross_out_grad: float32 [768, 768], P('dp')
- expand_grad: float32 [768, 3072], P('dp')
- contract_grad: float32 [3072, 768], P('dp')
- gain_one_grad: float32 [768], P('dp')
- shift_one_grad: float32 [768], P('dp')
- gain_two_grad: float32 [768], P('dp')
- shift_two_grad: float32 [768], P('dp')
- gain_three_grad: float32 [768], P('dp')
- shift_three_grad: float32 [768], P('dp')
Inputs may be any that keep to these rules, and one draw needn't show every extreme that they name: `lengths`: the number of valid memory tokens of each image; in each aligned block of 4 images one image has all 1280.
All inputs are finite; a program needn't handle non-finite values.
Results may differ from a plain program's by a relative error of at most 0.023.
Values may be sent and summed in bfloat16 or wider, within the bound.
A program may use at most 320 MiB of HBM per device.

v0:
```python
import jax
import jax.numpy as jnp
from jax import lax
from jax.sharding import PartitionSpec as P

H = 12
LOW = jnp.bfloat16
WIDE = jnp.float32


def mm(a, b, dims):
    return lax.dot_general(a, b, (dims, ((), ())), preferred_element_type=WIDE)


def project(values, weight):
    return mm(values, weight, ((1,), (0,)))


def back_project(grads, weight):
    return mm(grads, weight, ((1,), (1,)))


def weight_grad(left, right):
    return mm(left, right, ((0,), (0,)))


def heads_of(values, images):
    rows, width = values.shape
    return values.reshape(images, rows // images, H, width // H)


def norm_forward(resid, gain, shift):
    center = resid - jnp.mean(resid, axis=-1, keepdims=True)
    inverse = lax.rsqrt(jnp.mean(center * center, axis=-1, keepdims=True) + 1e-05)
    normed = center * inverse
    return (normed * gain + shift, normed, inverse)


def norm_backward(incoming, normed, inverse, gain):
    scaled = incoming * gain
    grad_in = inverse * (
        scaled
        - jnp.mean(scaled, axis=-1, keepdims=True)
        - normed * jnp.mean(scaled * normed, axis=-1, keepdims=True)
    )
    return (grad_in, jnp.sum(incoming * normed, axis=0), jnp.sum(incoming, axis=0))


def scores_of(query, keys):
    return jnp.einsum("bqhe,bkhe->bhqk", query, keys, preferred_element_type=WIDE) * 0.125


def mix(probs, values):
    return jnp.einsum("bhqk,bkhe->bqhe", probs, values, preferred_element_type=WIDE)


def mix_back(probs, grads):
    return jnp.einsum("bhqk,bqhe->bkhe", probs, grads, preferred_element_type=WIDE)


def attention_backward(probs, attn, grad_attn, query, keys, values):
    row = jnp.sum(grad_attn.astype(WIDE) * attn.astype(WIDE), axis=-1).transpose(0, 2, 1)[..., None]
    grad_probs = jnp.einsum("bqhe,bkhe->bhqk", grad_attn, values, preferred_element_type=WIDE)
    grad_scores = (probs * (grad_probs - row)).astype(LOW)
    grad_query = mix(grad_scores, keys) * 0.125
    grad_keys = mix_back(grad_scores, query) * 0.125
    grad_values = mix_back(probs.astype(LOW), grad_attn)
    return (grad_query, grad_keys, grad_values)


def gelu_tanh(values):
    return jax.nn.gelu(values, approximate=True)


def on_device(
    inputs,
    memory,
    lengths,
    self_query,
    self_key,
    self_value,
    self_out,
    cross_query,
    cross_key,
    cross_value,
    cross_out,
    expand_weight,
    contract_weight,
    gain_one,
    shift_one,
    gain_two,
    shift_two,
    gain_three,
    shift_three,
    cotangent,
):
    images, queries, width = inputs.shape
    mem_rows = memory.shape[1]
    rows = images * queries
    share = self_query.shape[0]
    parts = width // share
    squares = (
        self_query,
        self_key,
        self_value,
        self_out,
        cross_query,
        cross_key,
        cross_value,
        cross_out,
    )
    packed = lax.all_gather(jnp.stack(squares), "dp", axis=1, tiled=True)
    expand_full = lax.all_gather(expand_weight, "dp", axis=0, tiled=True)
    contract_full = lax.all_gather(contract_weight, "dp", axis=0, tiled=True)
    query_full, key_full, value_full, out_full, cquery_full, ckey_full, cvalue_full, cout_full = (
        packed
    )
    tokens = inputs.reshape(rows, width)
    memory_flat = memory.reshape(images * mem_rows, width)
    incoming = cotangent.reshape(rows, width).astype(WIDE)

    def joined(values):
        return values.reshape(-1, width)

    query_heads = heads_of(project(tokens, query_full).astype(LOW), images)
    key_heads = heads_of(project(tokens, key_full).astype(LOW), images)
    value_heads = heads_of(project(tokens, value_full).astype(LOW), images)
    self_raw = scores_of(query_heads, key_heads)
    self_exp = jnp.exp(self_raw - jnp.max(self_raw, axis=-1, keepdims=True))
    self_probs = self_exp / jnp.sum(self_exp, axis=-1, keepdims=True)
    self_attn = joined(mix(self_probs.astype(LOW), value_heads)).astype(LOW)
    first, normed_one, inverse_one = norm_forward(
        tokens.astype(WIDE) + project(self_attn, out_full), gain_one, shift_one
    )
    first_low = first.astype(LOW)
    cross_q = heads_of(project(first_low, cquery_full).astype(LOW), images)
    cross_k = heads_of(project(memory_flat, ckey_full).astype(LOW), images)
    cross_v = heads_of(project(memory_flat, cvalue_full).astype(LOW), images)
    places = lax.axis_index("mem") * mem_rows + jnp.arange(mem_rows, dtype=jnp.int32)
    valid = (places[None, :] < lengths[:, None])[:, None, None, :]
    cross_raw = jnp.where(valid, scores_of(cross_q, cross_k), -1e30)
    top = lax.pmax(jnp.max(cross_raw, axis=-1, keepdims=True), "mem")
    cross_exp = jnp.where(valid, jnp.exp(cross_raw - top), 0.0)
    total = lax.psum(jnp.sum(cross_exp, axis=-1, keepdims=True), "mem")
    cross_probs = cross_exp / total
    cross_attn = lax.psum(joined(mix(cross_probs.astype(LOW), cross_v)).astype(LOW), "mem")
    second, normed_two, inverse_two = norm_forward(
        first + project(cross_attn, cout_full), gain_two, shift_two
    )
    second_low = second.astype(LOW)
    pre_act = project(second_low, expand_full)
    activ, gelu_pull = jax.vjp(gelu_tanh, pre_act)
    activ_low = activ.astype(LOW)
    result, normed_three, inverse_three = norm_forward(
        second + project(activ_low, contract_full), gain_three, shift_three
    )
    grad_three, gain_three_part, shift_three_part = norm_backward(
        incoming, normed_three, inverse_three, gain_three
    )
    grad_ffn = grad_three.astype(LOW)

    def scattered(part, axes="dp"):
        return lax.psum_scatter(part, axes, scatter_dimension=0, tiled=True).astype(WIDE)

    contract_grad = scattered(weight_grad(activ_low, grad_ffn).astype(LOW))
    grad_pre = gelu_pull(back_project(grad_ffn, contract_full))[0].astype(LOW)
    expand_grad = scattered(weight_grad(second_low, grad_pre).astype(LOW))
    grad_second = grad_three + back_project(grad_pre, expand_full)
    grad_two, gain_two_part, shift_two_part = norm_backward(
        grad_second, normed_two, inverse_two, gain_two
    )
    grad_cross = grad_two.astype(LOW)
    cout_part = weight_grad(cross_attn, grad_cross)
    grad_cattn = heads_of(back_project(grad_cross, cout_full).astype(LOW), images)
    part_cquery, grad_ckey, grad_cvalue = attention_backward(
        cross_probs, heads_of(cross_attn, images), grad_cattn, cross_q, cross_k, cross_v
    )
    grad_cquery = lax.psum(joined(part_cquery).astype(LOW), "mem")
    grad_ckey = joined(grad_ckey).astype(LOW)
    grad_cvalue = joined(grad_cvalue).astype(LOW)
    kv_grad = scattered(
        jnp.concatenate(
            [weight_grad(memory_flat, grad_ckey), weight_grad(memory_flat, grad_cvalue)], axis=1
        ).astype(LOW),
        ("dp", "mem"),
    )
    memory_grad = back_project(grad_ckey, ckey_full) + back_project(grad_cvalue, cvalue_full)
    cquery_part = weight_grad(first_low, grad_cquery)
    grad_first = grad_two + back_project(grad_cquery, cquery_full)
    grad_one, gain_one_part, shift_one_part = norm_backward(
        grad_first, normed_one, inverse_one, gain_one
    )
    grad_self = grad_one.astype(LOW)
    out_part = weight_grad(self_attn, grad_self)
    grad_sattn = heads_of(back_project(grad_self, out_full).astype(LOW), images)
    grad_query, grad_key, grad_value = (
        joined(grad).astype(LOW)
        for grad in attention_backward(
            self_probs, heads_of(self_attn, images), grad_sattn, query_heads, key_heads, value_heads
        )
    )
    input_grad = (
        grad_one
        + back_project(grad_query, query_full)
        + back_project(grad_key, key_full)
        + back_project(grad_value, value_full)
    )
    norm_parts = jnp.stack(
        [
            gain_one_part,
            shift_one_part,
            gain_two_part,
            shift_two_part,
            gain_three_part,
            shift_three_part,
        ],
        axis=1,
    )
    rest = scattered(
        jnp.concatenate(
            [
                weight_grad(tokens, grad_query),
                weight_grad(tokens, grad_key),
                weight_grad(tokens, grad_value),
                out_part,
                cquery_part,
                cout_part,
                jnp.pad(norm_parts, ((0, 0), (0, 122))),
            ],
            axis=1,
        ).astype(LOW)
    )
    squares_grad = [rest[:, place * width : (place + 1) * width] for place in range(6)]
    norms_grad = [rest[:, 6 * width + place] for place in range(6)]
    return (
        result.reshape(inputs.shape),
        input_grad.reshape(inputs.shape),
        memory_grad.reshape(memory.shape),
        *squares_grad[:5],
        kv_grad[:, :width],
        kv_grad[:, width:],
        squares_grad[5],
        expand_grad,
        contract_grad,
        *norms_grad,
    )


def solution(mesh):
    rows = P("dp", None)
    image = P("dp", None, None)
    token = P("dp", "mem", None)
    both = P(("dp", "mem"), None)
    return jax.shard_map(
        on_device,
        mesh=mesh,
        in_specs=(image, token, P("dp"), *[rows] * 10, *[P()] * 6, image),
        out_specs=(image, image, token, *[rows] * 5, both, both, *[rows] * 3, *[P("dp")] * 6),
        check_vma=False,
    )
```

profile of v0, /device:TPU:0, one launch (start us, length us, event | category | flops | bytes accessed | tf_op | source)
XLA Modules:
  0.0 718.2 jit_solution(10065242548972240690)
XLA Ops:
  16.4 60.3 %all-gather.4.cloned.1.call-done = bf16[8,768,768]{2,1,0:T(8,128)(2,1)} async-done(((bf16[8,96,768]{2,1,0:T(8,128)(2,1)}), bf16[8,768,768]{2,1,0:T(8,128)(2,1)}) %all-gather.4.cloned.1.call-update) | async-done | bytes 9437200 | tf_op jit(solution)/shard_map/all_gather | solution.py:112
  76.7 4.3 fusion.11
  81.0 5.3 reshape.218
  90.1 3.0 copy.223
  99.2 3.0 fusion.59
  102.2 3.1 reshape.236
  107.6 3.3 fusion.89
  125.4 4.3 fusion.12
  129.7 5.1 reshape.220
  134.8 6.5 fusion.1
  141.3 19.0 %pmax.7 = f32[4,12,100]{2,1,0:T(8,128)S(1)} all-reduce(f32[4,12,100]{2,1,0:T(8,128)S(1)} %get-tuple-element.144), channel_id=1, replica_groups=mesh['dp'=8,'mem'=4] {'mem'}, use_global_device_ids=true, to_apply=%region_5.6 | all-reduce | flops 4800 | bytes 38400 | tf_op jit(solution)/shard_map/pmax | solution.py:142
  160.2 4.5 fusion.3
  164.7 15.9 %psum.21 = f32[4,12,100]{2,1,0:T(8,128)S(1)} all-reduce(f32[4,12,100]{2,1,0:T(8,128)S(1)} %fusion.3), channel_id=1, replica_groups=mesh['dp'=8,'mem'=4] {'mem'}, use_global_device_ids=true, to_apply=%region_7.8 | all-reduce | flops 4800 | bytes 38400 | tf_op jit(solution)/shard_map/psum | solution.py:144
  180.6 5.3 fusion.44
  196.0 36.2 %all-reduce.4.cloned.1.call-done = bf16[400,768]{0,1:T(8,128)(2,1)} async-done(((bf16[400,768]{0,1:T(8,128)(2,1)}), bf16[400,768]{0,1:T(8,128)(2,1)}) %all-reduce.4.cloned.1.call-update) | async-done | bytes 614416 | tf_op jit(solution)/shard_map/psum | solution.py:146
  236.2 36.1 %all-gather.6.cloned.1.call-done = bf16[768,3072]{1,0:T(8,128)(2,1)} async-done(((bf16[96,3072]{1,0:T(8,128)(2,1)}), bf16[768,3072]{1,0:T(8,128)(2,1)}) %all-gather.6.cloned.1.call-update) | async-done | bytes 4718608 | tf_op jit(solution)/shard_map/all_gather | solution.py:113
  272.3 7.2 fusion.79
  279.5 33.5 %all-gather.8.cloned.1.call-done = bf16[3072,768]{1,0:T(8,128)(2,1)} async-done(((bf16[384,768]{1,0:T(8,128)(2,1)}), bf16[3072,768]{1,0:T(8,128)(2,1)}) %all-gather.8.cloned.1.call-update) | async-done | bytes 4718608 | tf_op jit(solution)/shard_map/all_gather | solution.py:114
  313.0 7.3 %fusion.92 = (f32[400]{0:T(512)S(1)}, f32[400,768]{1,0:T(8,128)S(1)}) fusion(bf16[3072,768]{1,0:T(8,128)(2,1)} %all-gather.8.cloned.1.call-done, f32[400,3072]{1,0:T(8,128)} %fusion.79, f32[768]{0:T(1024)S(1)} %copy-done.43, f32[768]{0:T(1024)S(1)} %copy-done.38, f32[400]{0:T(512)S(1)} %add_rsqrt_fusion.1, f32[400,768]{1,0:T(8,128)} %copy-done.10, ...), kind=kOutput, calls=%fused_computation.172 | convolution fusion | flops 1900338816 | bytes 12102336 | tf_op jit(solution)/shard_map/dot_general | solution.py:12
  324.4 4.9 fusion.10
  333.4 2.8 convolution_convert_fusion.18
  338.4 3.0 reshape.222
  341.4 3.1 reshape.229
  346.7 6.6 multiply_convert_fusion
  358.0 4.5 convert_bitcast_fusion
  364.6 4.9 copy.254
  369.5 4.7 convert_element_type.257
  374.2 4.9 copy.256
  379.2 4.8 convert_element_type.260
  383.9 3.4 fusion.38
  390.6 4.3 copy.274
  395.0 7.0 convolution_convert_fusion.1
  402.3 8.0 %convolution_convert_fusion = bf16[3072,768]{1,0:T(8,128)(2,1)} fusion(f32[400,768]{1,0:T(8,128)} %copy-done.29, f32[400,3072]{1,0:T(8,128)} %fusion.79), kind=kOutput, calls=%fused_computation.9 | convolution fusion | flops 1901162496 | bytes 10862592 | tf_op jit(solution)/shard_map/dot_general | solution.py:12
  410.8 3.6 multiply_reduce_fusion.5
  417.7 3.1 reshape.238
  420.7 3.0 copy.240
  425.5 3.2 multiply_convert_fusion.3
  440.8 3.0 fusion.50
  448.0 3.2 fusion.32
  461.2 10.1 %copy.272 = bf16[768,4736]{1,0:T(8,128)(2,1)} copy(bf16[768,4736]{0,1:T(8,128)(2,1)} %pad_dynamic-update-slice_fusion) | data formatting | bytes 14548992
  473.8 3.0 copy.257
  476.8 3.2 fusion.62
  480.0 5.2 convolution_add_fusion
  489.6 3.2 convolution_add_fusion.1
  495.7 16.2 %reduce-scatter.15.cloned.1.call-done = bf16[24,1536]{1,0:T(8,128)(2,1)} async-done(((bf16[768,1536]{1,0:T(8,128)(2,1)}), bf16[24,1536]{1,0:T(8,128)(2,1)}) %reduce-scatter.15.cloned.1.call-update) | async-done | bytes 73744
  514.6 54.0 %reduce-scatter.9.cloned.1.call-done = bf16[96,3072]{1,0:T(8,128)(2,1)} async-done(((bf16[768,3072]{1,0:T(8,128)(2,1)}), bf16[96,3072]{1,0:T(8,128)(2,1)}) %reduce-scatter.9.cloned.1.call-update) | async-done | bytes 589840 | tf_op jit(solution)/shard_map/reduce_scatter | solution.py:163
  570.8 55.2 %reduce-scatter.11.cloned.1.call-done = bf16[384,768]{1,0:T(8,128)(2,1)} async-done(((bf16[3072,768]{1,0:T(8,128)(2,1)}), bf16[384,768]{1,0:T(8,128)(2,1)}) %reduce-scatter.11.cloned.1.call-update) | async-done | bytes 589840 | tf_op jit(solution)/shard_map/reduce_scatter | solution.py:163
  628.1 68.3 %reduce-scatter.13.cloned.1.call-done = bf16[96,4736]{1,0:T(8,128)(2,1)} async-done(((bf16[768,4736]{1,0:T(8,128)(2,1)}), bf16[96,4736]{1,0:T(8,128)(2,1)}) %reduce-scatter.13.cloned.1.call-update) | async-done | bytes 909328
  (231 shorter events, 135.7 us)
Async XLA Ops:
  7.2 69.5 %copy-start = (bf16[4,320,768]{2,1,0:T(8,128)(2,1)S(1)}, bf16[4,320,768]{2,1,0:T(8,128)(2,1)}, u32[]{:S(2)}) copy-start(bf16[4,320,768]{2,1,0:T(8,128)(2,1)} %param.21) | copy-start | bytes 5898244
  7.2 6.7 copy-start.35
  7.2 69.5 %all-gather.4.cloned.1.call-start = ((), (), s32[]{:S(2)}) async-start(), calls=%async_computation.4 | async-start | bytes 10616832 | tf_op jit(solution)/shard_map/all_gather | solution.py:112
  13.9 2.4 copy-start.40
  15.0 217.1 %all-reduce.4.cloned.1.call-start = ((), (), s32[]{:S(2)}) async-start(), calls=%async_computation.5 | async-start | bytes 1572864 | tf_op jit(solution)/shard_map/psum | solution.py:146
  16.3 82.9 %copy-start.33 = (bf16[400,768]{1,0:T(8,128)(2,1)}, bf16[400,768]{1,0:T(8,128)(2,1)S(1)}, u32[]{:S(2)}) copy-start(bf16[400,768]{1,0:T(8,128)(2,1)S(1)} %reshape.213) | copy-start | bytes 1843204
  99.2 8.4 %copy-start.14 = (bf16[4,100,12,64]{1,3,2,0:T(8,128)(2,1)}, bf16[4,100,12,64]{1,3,2,0:T(8,128)(2,1)S(1)}, u32[]{:S(2)}) copy-start(bf16[4,100,12,64]{1,3,2,0:T(8,128)(2,1)S(1)} %copy.221) | copy-start | bytes 1843204
  107.6 3.3 copy-start.15
  115.4 2.6 copy-start.30
  115.4 3.6 copy-start.39
  115.4 3.6 copy-start.44
  187.4 4.3 copy-start.3
  189.9 82.4 %all-gather.6.cloned.1.call-start = ((), (), s32[]{:S(2)}) async-start(), calls=%async_computation.6 | async-start | bytes 5308416 | tf_op jit(solution)/shard_map/all_gather | solution.py:113
  190.6 122.4 %all-gather.8.cloned.1.call-start = ((), (), s32[]{:S(2)}) async-start(), calls=%async_computation.7 | async-start | bytes 5308416 | tf_op jit(solution)/shard_map/all_gather | solution.py:114
  191.2 4.2 copy-start.36
  191.2 219.6 %all-reduce.6.cloned.1.call-start = ((), (), s32[]{:S(2)}) async-start(), calls=%async_computation.8 | async-start | bytes 1572864 | tf_op jit(solution)/shard_map/psum | solution.py:178
  196.0 76.3 %copy-start.38 = (f32[768]{0:T(1024)S(1)}, f32[768]{0:T(1024)}, u32[]{:S(2)}) copy-start(f32[768]{0:T(1024)} %param.35) | copy-start | bytes 9220
  196.0 76.3 %copy-start.43 = (f32[768]{0:T(1024)S(1)}, f32[768]{0:T(1024)}, u32[]{:S(2)}) copy-start(f32[768]{0:T(1024)} %param.36) | copy-start | bytes 9220
  313.0 10.7 %copy-start.46 = (f32[400,3072]{1,0:T(8,128)S(1)}, f32[400,3072]{1,0:T(8,128)}, u32[]{:S(2)}) copy-start(f32[400,3072]{1,0:T(8,128)} %fusion.79) | copy-start | bytes 14745604
  321.6 2.8 copy-start.41
  322.2 7.2 slice-start.2
  323.7 5.6 copy-start.29
  324.4 5.0 copy-start.11
  324.4 5.0 slice-start.3
  329.4 2.5 copy-start.47
  344.5 2.2 copy-start.13
  346.7 6.7 copy-start.1
  353.4 4.3 slice-start
  355.3 2.7 slice-start.1
  364.5 147.4 %reduce-scatter.15.cloned.1.call-start = ((), (), s32[]{:S(2)}) async-start(), calls=%async_computation.12 | async-start | bytes 2433024
  383.9 3.4 copy-start.22
  395.0 173.6 %reduce-scatter.9.cloned.1.call-start = ((), (), s32[]{:S(2)}) async-start(), calls=%async_computation.9 | async-start | bytes 5308416 | tf_op jit(solution)/shard_map/reduce_scatter | solution.py:163
  402.1 223.9 %reduce-scatter.11.cloned.1.call-start = ((), (), s32[]{:S(2)}) async-start(), calls=%async_computation.10 | async-start | bytes 5308416 | tf_op jit(solution)/shard_map/reduce_scatter | solution.py:163
  410.4 286.1 %reduce-scatter.13.cloned.1.call-start = ((), (), s32[]{:S(2)}) async-start(), calls=%async_computation.11 | async-start | bytes 8183808
  410.8 3.7 copy-start.6
  420.7 4.7 copy-start.45
  425.5 4.3 copy-start.16
  448.0 3.3 copy-start.18
  448.0 3.3 copy-start.34
  456.7 2.0 copy-start.32
  473.8 3.0 copy-start.23
  476.8 3.2 copy-start.24
  480.0 5.2 copy-start.17
  485.2 2.2 copy-start.19
  487.4 2.2 copy-start.21
  701.7 5.7 copy-start.27
  701.7 6.6 copy-start.26
  701.7 7.5 %copy-start.25 = (f32[96,768]{0,1:T(8,128)S(1)}, f32[96,768]{0,1:T(8,128)}, u32[]{:S(2)}) copy-start(f32[96,768]{0,1:T(8,128)} %get-tuple-element.132) | copy-start | bytes 884740
  (13 other events, 18.6 us)
Sparse Core Ops, SparseCore 0:
  15.1 61.5 all-gather.3
  190.0 42.0 all-reduce.3
  234.0 38.2 all-gather.5
  274.0 38.9 all-gather.7
  364.6 43.6 all-reduce.5
  413.5 98.3 reduce-scatter.14
  515.7 52.8 reduce-scatter.8
  572.1 53.8 reduce-scatter.10
  629.8 66.6 reduce-scatter.12
where the time goes:
time: 723 us; the launch traced here: 718 us
  waiting for transfers between devices  361 us (50%)
  matrix products  145 us (20%)
  local copies, waits for them, and re-layouts  141 us (20%)
  blocking collectives  34.8 us (5%)
  other arithmetic  20.4 us (3%)
  between operations  15 us (2%)
    reduce_scatter x2, waiting for transfers between devices, scattered(): lax.psum_scatter(part, axes, scatter_dimension=0, tiled=True).astype(WIDE)  109 us
    dot_general x30, matrix products, mm(): return lax.dot_general(a, b, (dims, ((), ())), preferred_element_type=WIDE)  102 us
    unnamed x11, waiting for transfers between devices  85.9 us
    all_gather x1, waiting for transfers between devices, on_device(): packed = lax.all_gather(jnp.stack(squares), 'dp', axis=1, tiled=True)  60.3 us
    unnamed x127, local copies, waits for them, and re-layouts  47.8 us
    reshape x13, local copies, waits for them, and re-layouts, heads_of(): return values.reshape(images, rows // images, H, width // H)  38.3 us
    psum x1, waiting for transfers between devices, on_device(): lax.psum(joined(mix(cross_probs.astype(LOW), cross_v)).astype(LOW), 'mem')  36.2 us
    all_gather x1, waiting for transfers between devices, on_device(): expand_full = lax.all_gather(expand_weight, 'dp', axis=0, tiled=True)  36.1 us
  transfers between devices with their start and end apart: 9, of which 8 were waited for; matrix products, arithmetic and copies ran while one was open for 21% of the time, Pallas kernels for 0%

commit v1 on v0

--- a/solution.py
+++ b/solution.py
@@ -6,6 +6,27 @@
 H = 12
 LOW = jnp.bfloat16
 WIDE = jnp.float32
+
+
+def collect(x, axis, dim):
+    size, index, span = (lax.axis_size(axis), lax.axis_index(axis), x.shape[dim])
+    ahead = [(i, (i + 1) % size) for i in range(size)]
+    left = [(i, (i - 1) % size) for i in range(size)]
+    whole = jnp.zeros((*x.shape[:dim], size * span, *x.shape[dim + 1 :]), x.dtype)
+    whole = lax.dynamic_update_slice_in_dim(whole, x, index * span, axis=dim)
+    from_left = from_right = x
+    halfway = size // 2
+    for turn in range(1, halfway + 1):
+        from_left = lax.ppermute(from_left, axis, ahead)
+        whole = lax.dynamic_update_slice_in_dim(
+            whole, from_left, (index - turn) % size * span, axis=dim
+        )
+        if turn < size - halfway:
+            from_right = lax.ppermute(from_right, axis, left)
+            whole = lax.dynamic_update_slice_in_dim(
+                whole, from_right, (index + turn) % size * span, axis=dim
+            )
+    return whole
 
 
 def mm(a, b, dims):
@@ -110,7 +131,7 @@
         cross_out,
     )
     packed = lax.all_gather(jnp.stack(squares), "dp", axis=1, tiled=True)
-    expand_full = lax.all_gather(expand_weight, "dp", axis=0, tiled=True)
+    expand_full = collect(expand_weight, "dp", 0)
     contract_full = lax.all_gather(contract_weight, "dp", axis=0, tiled=True)
     query_full, key_full, value_full, out_full, cquery_full, ckey_full, cvalue_full, cout_full = (
         packed

time: 723 us -> 690 us (0.954)
  waiting for transfers between devices: 361 us -> 304 us
  local copies, waits for them, and re-layouts: 141 us -> 154 us
  starting transfers between devices: 0.94 us -> 8.87 us
    ppermute x0 -> x7, waiting for transfers between devices: none -> 42.2 us  [the longest x4 42.2 us: collect(): from_left = lax.ppermute(from_left, axis, ahead)]
    psum x1, waiting for transfers between devices: 36.2 us -> 0.01 us  [on_device(): lax.psum(joined(mix(cross_probs.astype(LOW), cross_v)).astype(LOW), 'mem')]
    all_gather x1 -> x0, waiting for transfers between devices: 36.1 us -> none  [on_device(): expand_full = lax.all_gather(expand_weight, 'dp', axis=0, tiled=True)]
    all_gather x1, waiting for transfers between devices: 33.5 us -> 7.09 us  [on_device(): contract_full = lax.all_gather(contract_weight, 'dp', axis=0, tiled=True)]
    dynamic_update_slice x0 -> x8, local copies, waits for them, and re-layouts: none -> 8.98 us  [the longest x4 4.52 us: collect(): lax.dynamic_update_slice_in_dim(whole, from_left, (index - turn) % size *...]
    ppermute x0 -> x7, starting transfers between devices: none -> 8.37 us  [the longest x3 7.91 us: collect(): from_right = lax.ppermute(from_right, axis, left)]
    unnamed x127 -> x131, local copies, waits for them, and re-layouts: 47.8 us -> 49.1 us
    unnamed x11 -> x10, waiting for transfers between devices: 85.9 us -> 85.3 us
  transfers between devices with their start and end apart: 9 -> 15, of which waited for: 8 -> 10; matrix products, arithmetic and copies ran while one was open for 21% -> 24% of each run, Pallas kernels for 0% -> 0%
where the time goes in v1:
time: 690 us; the launch traced here: 685 us
  waiting for transfers between devices  304 us (44%)
  local copies, waits for them, and re-layouts  154 us (22%)
  matrix products  148 us (21%)
  blocking collectives  34.8 us (5%)
  other arithmetic  20.3 us (3%)
  between operations  15.3 us (2%)
  starting transfers between devices  8.87 us (1%)
    reduce_scatter x2, waiting for transfers between devices, scattered(): lax.psum_scatter(part, axes, scatter_dimension=0, tiled=True).astype(WIDE)  109 us
    dot_general x30, matrix products, mm(): return lax.dot_general(a, b, (dims, ((), ())), preferred_element_type=WIDE)  106 us
    unnamed x10, waiting for transfers between devices  85.3 us
    all_gather x1, waiting for transfers between devices, on_device(): packed = lax.all_gather(jnp.stack(squares), 'dp', axis=1, tiled=True)  60.3 us
    unnamed x131, local copies, waits for them, and re-layouts  49.1 us
    ppermute x4, waiting for transfers between devices, collect(): from_left = lax.ppermute(from_left, axis, ahead)  42.2 us
    reshape x13, local copies, waits for them, and re-layouts, heads_of(): return values.reshape(images, rows // images, H, width // H)  38.3 us
    pmax x1, blocking collectives, on_device(): top = lax.pmax(jnp.max(cross_raw, axis=-1, keepdims=True), 'mem')  19 us
  transfers between devices with their start and end apart: 15, of which 10 were waited for; matrix products, arithmetic and copies ran while one was open for 24% of the time, Pallas kernels for 0%

profile of v1, /device:TPU:0, one launch (start us, length us, event | category | flops | bytes accessed | tf_op | source)
XLA Modules:
  0.0 685.5 jit_solution(7074112221354108882)
XLA Ops:
  16.4 60.3 %all-gather.3.cloned.1.call-done = bf16[8,768,768]{2,1,0:T(8,128)(2,1)} async-done(((bf16[8,96,768]{2,1,0:T(8,128)(2,1)}), bf16[8,768,768]{2,1,0:T(8,128)(2,1)}) %all-gather.3.cloned.1.call-update) | async-done | bytes 9437200 | tf_op jit(solution)/shard_map/all_gather | solution.py:133
  76.7 4.3 fusion.11
  81.0 5.3 reshape.218
  99.2 3.0 fusion.59
  102.2 3.1 reshape.236
  107.6 3.3 fusion.89
  125.4 4.3 fusion.12
  129.7 5.1 reshape.220
  134.8 6.4 fusion.1
  141.2 19.0 %pmax.7 = f32[4,12,100]{2,1,0:T(8,128)S(1)} all-reduce(f32[4,12,100]{2,1,0:T(8,128)S(1)} %get-tuple-element.144), channel_id=1, replica_groups=mesh['dp'=8,'mem'=4] {'mem'}, use_global_device_ids=true, to_apply=%region_5.6 | all-reduce | flops 4800 | bytes 38400 | tf_op jit(solution)/shard_map/pmax | solution.py:163
  160.2 4.4 fusion.3
  164.7 15.9 %psum.21 = f32[4,12,100]{2,1,0:T(8,128)S(1)} all-reduce(f32[4,12,100]{2,1,0:T(8,128)S(1)} %fusion.3), channel_id=1, replica_groups=mesh['dp'=8,'mem'=4] {'mem'}, use_global_device_ids=true, to_apply=%region_7.8 | all-reduce | flops 4800 | bytes 38400 | tf_op jit(solution)/shard_map/psum | solution.py:165
  181.1 5.3 fusion.44
  201.8 5.5 collective-permute-done
  213.7 10.0 %collective-permute-done.2 = bf16[96,3072]{1,0:T(8,128)(2,1)S(1)} collective-permute-done((bf16[96,3072]{1,0:T(8,128)(2,1)}, bf16[96,3072]{1,0:T(8,128)(2,1)S(1)}, u32[]{:S(2)}, u32[]{:S(2)}) %collective-permute-start.2) | collective-permute-done | bytes 589856 | tf_op jit(solution)/shard_map/ppermute | solution.py:20
  228.1 11.9 %collective-permute-done.4 = bf16[96,3072]{1,0:T(8,128)(2,1)S(1)} collective-permute-done((bf16[96,3072]{1,0:T(8,128)(2,1)S(1)}, bf16[96,3072]{1,0:T(8,128)(2,1)S(1)}, u32[]{:S(2)}, u32[]{:S(2)}) %collective-permute-start.4) | collective-permute-done | bytes 589856 | tf_op jit(solution)/shard_map/ppermute | solution.py:20
  242.1 14.8 %collective-permute-done.6 = bf16[96,3072]{1,0:T(8,128)(2,1)S(1)} collective-permute-done((bf16[96,3072]{1,0:T(8,128)(2,1)S(1)}, bf16[96,3072]{1,0:T(8,128)(2,1)S(1)}, u32[]{:S(2)}, u32[]{:S(2)}) %collective-permute-start.6) | collective-permute-done | bytes 589856 | tf_op jit(solution)/shard_map/ppermute | solution.py:20
  257.8 3.0 fusion.91
  261.9 6.8 fusion.79
  268.7 7.1 %all-gather.5.cloned.1.call-done = bf16[3072,768]{1,0:T(8,128)(2,1)} async-done(((bf16[384,768]{1,0:T(8,128)(2,1)}), bf16[3072,768]{1,0:T(8,128)(2,1)}) %all-gather.5.cloned.1.call-update) | async-done | bytes 4718608 | tf_op jit(solution)/shard_map/all_gather | solution.py:135
  275.8 7.3 %fusion.92 = (f32[400]{0:T(512)S(1)}, f32[400,768]{1,0:T(8,128)S(1)}) fusion(bf16[3072,768]{1,0:T(8,128)(2,1)} %all-gather.5.cloned.1.call-done, f32[400,3072]{1,0:T(8,128)} %fusion.79, f32[768]{0:T(1024)S(1)} %copy-done.46, f32[768]{0:T(1024)S(1)} %copy-done.41, f32[400]{0:T(512)S(1)} %add_rsqrt_fusion.1, f32[400,768]{1,0:T(8,128)} %copy-done.10, ...), kind=kOutput, calls=%fused_computation.180 | convolution fusion | flops 1900338816 | bytes 12102336 | tf_op jit(solution)/shard_map/dot_general | solution.py:33
  288.2 4.9 fusion.10
  293.1 5.8 multiply_reduce_fusion.4
  308.5 3.1 reshape.229
  313.8 6.7 multiply_convert_fusion
  325.0 4.5 convert_bitcast_fusion
  331.6 4.9 copy.254
  336.5 4.7 convert_element_type.257
  341.3 5.0 copy.256
  346.2 4.8 convert_element_type.260
  351.0 3.4 fusion.38
  357.7 4.3 copy.274
  362.1 7.1 %convolution_convert_fusion.1 = bf16[768,3072]{1,0:T(8,128)(2,1)} fusion(bf16[400,3072]{1,0:T(8,128)(2,1)} %copy-done.51, f32[400,768]{1,0:T(8,128)} %copy-done.10, f32[768]{0:T(1024)S(1)} %copy-done.46, f32[768]{0:T(1024)S(1)} %copy-done.41, f32[400]{0:T(512)S(1)} %add_rsqrt_fusion.1, f32[400]{0:T(512)S(1)} %broadcast_multiply_fusion.7), kind=kOutput, calls=%fused_computation.10 | convolution fusion | flops 1891332096 | bytes 8414336 | tf_op jit(solution)/shard_map/dot_general | solution.py:33
  369.4 8.0 %convolution_convert_fusion = bf16[3072,768]{1,0:T(8,128)(2,1)} fusion(f32[400,768]{1,0:T(8,128)} %copy-done.29, f32[400,3072]{1,0:T(8,128)} %fusion.79), kind=kOutput, calls=%fused_computation.9 | convolution fusion | flops 1901162496 | bytes 10862592 | tf_op jit(solution)/shard_map/dot_general | solution.py:33
  377.9 3.6 multiply_reduce_fusion.5
  384.7 3.1 reshape.238
  387.8 3.0 copy.240
  392.6 3.2 multiply_convert_fusion.3
  407.8 3.0 fusion.50
  415.0 3.3 fusion.32
  428.3 10.1 %copy.272 = bf16[768,4736]{1,0:T(8,128)(2,1)} copy(bf16[768,4736]{0,1:T(8,128)(2,1)} %pad_dynamic-update-slice_fusion) | data formatting | bytes 14548992
  443.9 3.2 fusion.62
  447.1 5.2 convolution_add_fusion
  456.7 3.2 convolution_add_fusion.1
  462.8 16.2 %reduce-scatter.15.cloned.1.call-done = bf16[24,1536]{1,0:T(8,128)(2,1)} async-done(((bf16[768,1536]{1,0:T(8,128)(2,1)}), bf16[24,1536]{1,0:T(8,128)(2,1)}) %reduce-scatter.15.cloned.1.call-update) | async-done | bytes 73744
  481.6 53.9 %reduce-scatter.9.cloned.1.call-done = bf16[96,3072]{1,0:T(8,128)(2,1)} async-done(((bf16[768,3072]{1,0:T(8,128)(2,1)}), bf16[96,3072]{1,0:T(8,128)(2,1)}) %reduce-scatter.9.cloned.1.call-update) | async-done | bytes 589840 | tf_op jit(solution)/shard_map/reduce_scatter | solution.py:184
  537.7 55.2 %reduce-scatter.11.cloned.1.call-done = bf16[384,768]{1,0:T(8,128)(2,1)} async-done(((bf16[3072,768]{1,0:T(8,128)(2,1)}), bf16[384,768]{1,0:T(8,128)(2,1)}) %reduce-scatter.11.cloned.1.call-update) | async-done | bytes 589840 | tf_op jit(solution)/shard_map/reduce_scatter | solution.py:184
  595.0 68.3 %reduce-scatter.13.cloned.1.call-done = bf16[96,4736]{1,0:T(8,128)(2,1)} async-done(((bf16[768,4736]{1,0:T(8,128)(2,1)}), bf16[96,4736]{1,0:T(8,128)(2,1)}) %reduce-scatter.13.cloned.1.call-update) | async-done | bytes 909328
  (254 shorter events, 162.6 us)
Async XLA Ops:
  7.2 69.5 %copy-start = (bf16[4,320,768]{2,1,0:T(8,128)(2,1)S(1)}, bf16[4,320,768]{2,1,0:T(8,128)(2,1)}, u32[]{:S(2)}) copy-start(bf16[4,320,768]{2,1,0:T(8,128)(2,1)} %param.21) | copy-start | bytes 5898244
  7.2 6.7 copy-start.36
  7.2 69.5 %all-gather.3.cloned.1.call-start = ((), (), s32[]{:S(2)}) async-start(), calls=%async_computation.4 | async-start | bytes 10616832 | tf_op jit(solution)/shard_map/all_gather | solution.py:133
  15.0 242.8 %all-reduce.4.cloned.1.call-start = ((), (), s32[]{:S(2)}) async-start(), calls=%async_computation.5 | async-start | bytes 1572864 | tf_op jit(solution)/shard_map/psum | solution.py:167
  16.3 82.9 %copy-start.33 = (bf16[400,768]{1,0:T(8,128)(2,1)}, bf16[400,768]{1,0:T(8,128)(2,1)S(1)}, u32[]{:S(2)}) copy-start(bf16[400,768]{1,0:T(8,128)(2,1)S(1)} %reshape.213) | copy-start | bytes 1843204
  99.2 8.4 %copy-start.14 = (bf16[4,100,12,64]{1,3,2,0:T(8,128)(2,1)}, bf16[4,100,12,64]{1,3,2,0:T(8,128)(2,1)S(1)}, u32[]{:S(2)}) copy-start(bf16[4,100,12,64]{1,3,2,0:T(8,128)(2,1)S(1)} %copy.221) | copy-start | bytes 1843204
  107.6 3.3 copy-start.15
  115.3 3.6 copy-start.42
  115.3 3.6 copy-start.47
  186.4 7.5 %copy-start.3 = (bf16[4,100,768]{2,0,1:T(4,128)(2,1)S(1)}, bf16[4,100,768]{2,0,1:T(4,128)(2,1)}, u32[]{:S(2)}) copy-start(bf16[4,100,768]{2,0,1:T(4,128)(2,1)} %param.39) | copy-start | bytes 1843204
  186.4 7.5 %copy-start.37 = (f32[768]{0:T(1024)S(1)}, f32[768]{0:T(1024)}, u32[]{:S(2)}) copy-start(f32[768]{0:T(1024)} %param.37) | copy-start | bytes 9220
  190.4 85.4 %all-gather.5.cloned.1.call-start = ((), (), s32[]{:S(2)}) async-start(), calls=%async_computation.6 | async-start | bytes 5308416 | tf_op jit(solution)/shard_map/all_gather | solution.py:135
  191.1 186.7 %all-reduce.6.cloned.1.call-start = ((), (), s32[]{:S(2)}) async-start(), calls=%async_computation.7 | async-start | bytes 1572864 | tf_op jit(solution)/shard_map/psum | solution.py:199
  191.2 16.1 %collective-permute-start = (bf16[96,3072]{1,0:T(8,128)(2,1)}, bf16[96,3072]{1,0:T(8,128)(2,1)}, u32[]{:S(2)}, u32[]{:S(2)}) collective-permute-start(bf16[96,3072]{1,0:T(8,128)(2,1)} %param.31), channel_id=1, source_target_pairs={{0,4},{4,8},{8,12},{12,16},{16,20},{20,24},{24,28},{28,0},{1,5},{5... | collective-permute-start | bytes 1769480 | tf_op jit(solution)/shard_map/ppermute | solution.py:20
  191.2 16.0 %collective-permute-start.1 = (bf16[96,3072]{1,0:T(8,128)(2,1)}, bf16[96,3072]{1,0:T(8,128)(2,1)}, u32[]{:S(2)}, u32[]{:S(2)}) collective-permute-start(bf16[96,3072]{1,0:T(8,128)(2,1)} %param.31), channel_id=1, source_target_pairs={{0,28},{4,0},{8,4},{12,8},{16,12},{20,16},{24,20},{28,24},{1,29},{... | collective-permute-start | bytes 1769480 | tf_op jit(solution)/shard_map/ppermute | solution.py:25
  198.1 2.8 copy-start.35
  207.2 16.5 %collective-permute-start.2 = (bf16[96,3072]{1,0:T(8,128)(2,1)}, bf16[96,3072]{1,0:T(8,128)(2,1)S(1)}, u32[]{:S(2)}, u32[]{:S(2)}) collective-permute-start(bf16[96,3072]{1,0:T(8,128)(2,1)} %collective-permute-done), channel_id=1, source_target_pairs={{0,4},{4,8},{8,12},{12,16},{16,20},{20,24},{24,28},{28,0},{1,5},{5... | collective-permute-start | bytes 1769480 | tf_op jit(solution)/shard_map/ppermute | solution.py:20
  207.2 16.5 %collective-permute-start.3 = (bf16[96,3072]{1,0:T(8,128)(2,1)}, bf16[96,3072]{1,0:T(8,128)(2,1)S(1)}, u32[]{:S(2)}, u32[]{:S(2)}) collective-permute-start(bf16[96,3072]{1,0:T(8,128)(2,1)} %collective-permute-done.1), channel_id=1, source_target_pairs={{0,28},{4,0},{8,4},{12,8},{16,12},{20,16},{24,20},{28,24},{1,29},{... | collective-permute-start | bytes 1769480 | tf_op jit(solution)/shard_map/ppermute | solution.py:25
  223.7 16.3 %collective-permute-start.4 = (bf16[96,3072]{1,0:T(8,128)(2,1)S(1)}, bf16[96,3072]{1,0:T(8,128)(2,1)S(1)}, u32[]{:S(2)}, u32[]{:S(2)}) collective-permute-start(bf16[96,3072]{1,0:T(8,128)(2,1)S(1)} %collective-permute-done.2), channel_id=1, source_target_pairs={{0,4},{4,8},{8,12},{12,16},{16,20},{20,24},{24,28},{28,0},{1,5},{5... | collective-permute-start | bytes 1769480 | tf_op jit(solution)/shard_map/ppermute | solution.py:20
  223.8 17.5 %collective-permute-start.5 = (bf16[96,3072]{1,0:T(8,128)(2,1)S(1)}, bf16[96,3072]{1,0:T(8,128)(2,1)S(1)}, u32[]{:S(2)}, u32[]{:S(2)}) collective-permute-start(bf16[96,3072]{1,0:T(8,128)(2,1)S(1)} %collective-permute-done.3), channel_id=1, source_target_pairs={{0,28},{4,0},{8,4},{12,8},{16,12},{20,16},{24,20},{28,24},{1,29},{... | collective-permute-start | bytes 1769480 | tf_op jit(solution)/shard_map/ppermute | solution.py:25
  228.1 29.7 %copy-start.48 = (f32[768]{0:T(1024)S(1)}, f32[768]{0:T(1024)}, u32[]{:S(2)}) copy-start(f32[768]{0:T(1024)} %param.34) | copy-start | bytes 9220
  240.0 16.9 %collective-permute-start.6 = (bf16[96,3072]{1,0:T(8,128)(2,1)S(1)}, bf16[96,3072]{1,0:T(8,128)(2,1)S(1)}, u32[]{:S(2)}, u32[]{:S(2)}) collective-permute-start(bf16[96,3072]{1,0:T(8,128)(2,1)S(1)} %collective-permute-done.4), channel_id=1, source_target_pairs={{0,4},{4,8},{8,12},{12,16},{16,20},{20,24},{24,28},{28,0},{1,5},{5... | collective-permute-start | bytes 1769480 | tf_op jit(solution)/shard_map/ppermute | solution.py:20
  257.8 4.1 copy-start.41
  257.8 4.1 copy-start.46
  275.8 10.7 %copy-start.50 = (f32[400,3072]{1,0:T(8,128)S(1)}, f32[400,3072]{1,0:T(8,128)}, u32[]{:S(2)}) copy-start(f32[400,3072]{1,0:T(8,128)} %fusion.79) | copy-start | bytes 14745604
  284.9 3.2 copy-start.44
  286.5 6.7 copy-start.29
  288.2 5.0 copy-start.11
  293.1 5.8 copy-start.51
  308.5 5.3 copy-start.39
  313.8 6.7 copy-start.1
  320.5 4.3 slice-start
  331.5 147.4 %reduce-scatter.15.cloned.1.call-start = ((), (), s32[]{:S(2)}) async-start(), calls=%async_computation.11 | async-start | bytes 2433024
  351.0 3.4 copy-start.22
  362.0 173.5 %reduce-scatter.9.cloned.1.call-start = ((), (), s32[]{:S(2)}) async-start(), calls=%async_computation.8 | async-start | bytes 5308416 | tf_op jit(solution)/shard_map/reduce_scatter | solution.py:184
  369.2 223.7 %reduce-scatter.11.cloned.1.call-start = ((), (), s32[]{:S(2)}) async-start(), calls=%async_computation.9 | async-start | bytes 5308416 | tf_op jit(solution)/shard_map/reduce_scatter | solution.py:184
  377.4 285.9 %reduce-scatter.13.cloned.1.call-start = ((), (), s32[]{:S(2)}) async-start(), calls=%async_computation.10 | async-start | bytes 8183808
  377.9 3.7 copy-start.6
  387.8 4.8 copy-start.49
  392.6 4.3 copy-start.16
  415.0 3.3 copy-start.18
  415.0 3.3 copy-start.34
  440.9 3.0 copy-start.23
  443.9 3.2 copy-start.24
  447.1 5.2 copy-start.17
  668.6 5.7 copy-start.27
  668.6 6.6 copy-start.26
  668.6 7.5 %copy-start.25 = (f32[96,768]{0,1:T(8,128)S(1)}, f32[96,768]{0,1:T(8,128)}, u32[]{:S(2)}) copy-start(f32[96,768]{0,1:T(8,128)} %get-tuple-element.132) | copy-start | bytes 884740
  (21 other events, 35.6 us)
Sparse Core Ops, SparseCore 0:
  15.1 61.5 all-gather.2
  190.5 42.0 all-reduce.3
  234.5 41.1 all-gather.4
  331.7 43.6 all-reduce.5
  380.5 98.3 reduce-scatter.14
  482.6 52.8 reduce-scatter.8
  539.0 53.8 reduce-scatter.10
  596.7 66.6 reduce-scatter.12
